TPU v7x, 256 devices: a whole 4x4x8 slice. The times are simulated.
256 devices in a mesh: illum: 32 (over z_hi, x, y), row: 8 (over z_lo, core).
Axes of the slice: x: 4, y: 4, z: 8 (z_hi: 2, z_lo: 4; z = z_hi * 4 + z_lo), core: 2. Of those that a mesh axis runs over, the one named last changes fastest.
Arguments:
- angles: int32 [128, 2], P('illum'), may hold values from -8 to 8
- depth_order: int32 [3], replicated, may hold values from 0 to 31, as said below
- slices: float32 [32, 64, 4096], P('illum', 'row'), may hold values from -4 to 4
- cotangent: float32 [128, 2, 64, 4096], P('illum', None, 'row'), may hold values from -0.6 to 0.6
Outputs:
- exit_field: float32 [128, 2, 64, 4096], P('illum', None, 'row')
- slice_grad: float32 [32, 64, 4096], P('illum', 'row')
Inputs may be any that keep to these rules, and one draw needn't show every extreme that they name: `depth_order`: 3 distinct slice numbers; slice 0 and the last slice are always among them.
All inputs are finite; a program needn't handle non-finite values.
Results may differ from a plain program's by a relative error of at most 0.0001.
Values sent between devices are 32-bit elements; how exact they have to be, the bound alone decides.
No kernel may reach another device: no remote copies, remote signals or barrier semaphores. Data moves between devices by JAX's collectives and lax.ppermute only.
A program may use at most 64 MiB of HBM per device.

v0:
```python
import math
import jax
import jax.numpy as jnp
from jax import lax
from jax.sharding import PartitionSpec as P

rate_scale = 0.3


def extended(array, sides, width):
    for axis, dim in sides:
        peers, length = (lax.axis_size(axis), array.shape[dim])
        up = [(i, (i + 1) % peers) for i in range(peers - 1)]
        down = [(j, i) for i, j in up]
        last = lax.slice_in_dim(array, length - width, length, axis=dim)
        initial = lax.slice_in_dim(array, 0, width, axis=dim)
        before = lax.ppermute(last, axis, up)
        after = lax.ppermute(initial, axis, down)
        array = jnp.concatenate([before, array, after], axis=dim)
    return array


def broadcast(block, axis, holder):
    block = jnp.where(lax.axis_index(axis) == holder, block, jnp.zeros_like(block))
    return lax.psum(block, axis)


def laplace_padded(padded):
    framed = jnp.pad(padded, ((0, 0), (0, 0), (0, 0), (1, 1)))
    centre = framed[:, :, 1:-1, 1:-1]
    return (
        framed[:, :, 2:, 1:-1]
        + framed[:, :, :-2, 1:-1]
        + (framed[:, :, 1:-1, 2:] + framed[:, :, 1:-1, :-2])
        - 4.0 * centre
    )


def forward_rate(field):
    padded = extended(field, (("row", 2),), 1)
    curved = laplace_padded(padded)
    return jnp.stack([-rate_scale * curved[:, 1], rate_scale * curved[:, 0]], axis=1)


def adjoint_rate(field):
    padded = extended(field, (("row", 2),), 1)
    curved = laplace_padded(padded)
    factor = -rate_scale
    return jnp.stack([-factor * curved[:, 1], factor * curved[:, 0]], axis=1)


def runge_step(field, rate_fn):
    slope_one = rate_fn(field)
    slope_two = rate_fn(field + 0.5 * slope_one)
    slope_three = rate_fn(field + 0.5 * slope_two)
    slope_four = rate_fn(field + slope_three)
    return field + (slope_one + 2.0 * slope_two + 2.0 * slope_three + slope_four) / 6.0


def rotate(field, phase):
    cosine = jnp.cos(phase)
    sine = jnp.sin(phase)
    real_part = field[:, 0]
    imag_part = field[:, 1]
    return jnp.stack(
        [cosine * real_part - sine * imag_part, sine * real_part + cosine * imag_part], axis=1
    )


def inner_term(adjoint, stored):
    return jnp.sum(-adjoint[:, 0] * stored[:, 1] + adjoint[:, 1] * stored[:, 0], axis=0)


def body(angles, depth_order, slices, cotangent):
    rows = slices.shape[1]
    cols = slices.shape[2]
    layers = depth_order.shape[0]
    owner_count = lax.axis_size("illum")
    total_rows = rows * lax.axis_size("row")
    first_row = lax.axis_index("row") * rows
    rows_idx = first_row + jnp.arange(rows, dtype=jnp.int32)
    cols_idx = jnp.arange(cols, dtype=jnp.int32)
    phase_rows = (
        2.0
        * math.pi
        * (angles[:, 0:1] * rows_idx[None, :] % total_rows).astype(jnp.float32)
        / total_rows
    )
    phase_cols = (
        2.0 * math.pi * (angles[:, 1:2] * cols_idx[None, :] % cols).astype(jnp.float32) / cols
    )
    phase = phase_rows[:, :, None] + phase_cols[:, None, :]
    field = jnp.stack([jnp.cos(phase), jnp.sin(phase)], axis=1)
    chosen = [broadcast(slices[0], "illum", depth_order[layer]) for layer in range(layers)]
    kept = [None] * layers
    terms = [None] * layers
    adjoint = cotangent
    for layer in range(layers):
        field = rotate(field, chosen[layer])
        kept[layer] = field
        field = runge_step(field, forward_rate)
    for layer in range(layers - 1, -1, -1):
        adjoint = runge_step(adjoint, adjoint_rate)
        terms[layer] = inner_term(adjoint, kept[layer])
        adjoint = rotate(adjoint, -chosen[layer])
    grads = jnp.stack(terms, axis=0)
    owners = jnp.arange(owner_count, dtype=jnp.int32)
    buffer = jnp.zeros((owner_count, rows, cols), jnp.float32)
    for layer in range(layers):
        picked = (owners == depth_order[layer]).astype(jnp.float32)
        buffer = buffer + picked[:, None, None] * grads[layer][None]
    slice_grad = lax.psum_scatter(buffer, "illum", scatter_dimension=0, tiled=True)
    return (field, slice_grad)


def solution(mesh):
    placed = (P("illum", None), P(), P("illum", "row", None), P("illum", None, "row", None))
    return jax.shard_map(
        body,
        mesh=mesh,
        in_specs=placed,
        out_specs=(P("illum", None, "row", None), P("illum", "row", None)),
        check_vma=False,
    )
```

profile of v0, /device:TPU:32, one launch (start us, length us, event | category | flops | bytes accessed | tf_op | source)
XLA Modules:
  0.0 844.7 jit_solution(2397940869130016920)
XLA Ops:
  7.2 1.9 copy.96
  9.2 1.9 collective-permute-start.24
  11.1 2.4 collective-permute-start.25
  21.2 2.8 collective-permute-start.26
  24.0 2.0 collective-permute-start.27
  26.5 3.8 collective-permute-done.27
  33.0 1.9 collective-permute-start.28
  34.9 2.4 collective-permute-start.29
  39.2 2.0 collective-permute-done.29
  46.5 2.4 collective-permute-start.31
  48.9 386.7 %all-reduce.27.cloned.1.call-done = (f32[8,4096]{1,0:T(8,128)}, f32[8,4096]{1,0:T(8,128)}, f32[8,4096]{1,0:T(8,128)}) async-done(((f32[8,4096]{1,0:T(8,128)}, f32[8,4096]{1,0:T(8,128)}, f32[8,4096]{1,0:T(8,128)}), (f32[8,4096]{1,0:T(8,128)}, f32[8,4096]{1,0:T(8,128)}, f32[8,4096]{1,0:T(8,128)})) %all-reduce.27.cloned.1.call-update) | async-done | bytes 393232 | tf_op jit(solution)/shard_map/psum | solution.py:25
  437.0 4.2 fusion.105
  441.3 1.9 collective-permute-start
  443.2 2.6 collective-permute-start.1
  452.7 3.2 collective-permute-start.32
  455.8 1.9 collective-permute-start.33
  460.3 3.6 collective-permute-start.2
  464.0 1.9 collective-permute-start.3
  468.5 3.6 collective-permute-start.34
  476.3 3.6 collective-permute-start.4
  479.9 2.3 collective-permute-start.5
  484.5 3.6 collective-permute-start.36
  488.1 1.9 collective-permute-start.37
  492.2 3.6 collective-permute-start.6
  500.0 3.6 collective-permute-start.38
  508.9 3.6 collective-permute-start.8
  512.5 2.1 collective-permute-start.9
  517.9 3.6 collective-permute-start.40
  521.5 1.9 collective-permute-start.41
  526.1 3.6 collective-permute-start.10
  535.0 3.6 collective-permute-start.42
  542.7 3.6 collective-permute-start.12
  546.4 2.1 collective-permute-start.13
  550.7 3.6 collective-permute-start.44
  554.4 1.9 collective-permute-start.45
  558.5 3.6 collective-permute-start.14
  566.2 3.6 collective-permute-start.46
  575.1 3.6 collective-permute-start.16
  578.8 2.2 collective-permute-start.17
  584.6 4.7 fusion.117
  592.6 3.6 collective-permute-start.18
  598.1 2.9 multiply_add_fusion
  604.7 2.2 collective-permute-start.20
  607.0 2.1 collective-permute-start.21
  609.5 4.5 collective-permute-done.21
  618.1 2.7 collective-permute-start.23
  620.8 6.2 collective-permute-done.23
  631.5 205.9 %reduce-scatter.2.cloned.1.call-done = f32[1,8,4096]{2,1,0:T(8,128)} async-done(((f32[32,8,4096]{2,1,0:T(8,128)}), f32[1,8,4096]{2,1,0:T(8,128)}) %reduce-scatter.2.cloned.1.call-update) | async-done | bytes 131088 | tf_op jit(solution)/shard_map/reduce_scatter | solution.py:112
  (223 shorter events, 96.5 us)
Async XLA Ops:
  7.2 428.4 %all-reduce.27.cloned.1.call-start = ((), (), s32[]{:S(2)}) async-start(), calls=%async_computation.2 | async-start | bytes 786432 | tf_op jit(solution)/shard_map/psum | solution.py:25
  9.2 7.8 collective-permute-start.24
  11.1 6.5 collective-permute-start.25
  16.8 820.6 %reduce-scatter.2.cloned.1.call-start = ((), (), s32[]{:S(2)}) async-start(), calls=%async_computation.1 | async-start | bytes 4325376 | tf_op jit(solution)/shard_map/reduce_scatter | solution.py:112
  21.2 5.3 collective-permute-start.26
  24.0 6.3 collective-permute-start.27
  33.0 6.2 collective-permute-start.28
  34.9 6.3 collective-permute-start.29
  44.6 403.2 %collective-permute-start.30 = (f32[4,2,1,4096]{3,0,2,1:T(4,128)}, f32[4,2,1,4096]{3,0,2,1:T(4,128)S(1)}, u32[]{:S(2)}, u32[]{:S(2)}) collective-permute-start(f32[4,2,1,4096]{3,0,2,1:T(4,128)} %get-tuple-element.50), channel_id=1, source_target_pairs={{1,0},{2,1},{3,2},{4,3},{5,4},{6,5},{7,6},{9,8},{10,9},{11,10},{12... | collective-permute-start | bytes 393224 | tf_op jit(solution)/shard_map/ppermute | solution.py:18
  46.5 401.3 %collective-permute-start.31 = (f32[4,2,1,4096]{3,0,2,1:T(4,128)}, f32[4,2,1,4096]{3,0,2,1:T(4,128)S(1)}, u32[]{:S(2)}, u32[]{:S(2)}) collective-permute-start(f32[4,2,1,4096]{3,0,2,1:T(4,128)} %get-tuple-element.49), channel_id=1, source_target_pairs={{0,1},{1,2},{2,3},{3,4},{4,5},{5,6},{6,7},{8,9},{9,10},{10,11},{11... | collective-permute-start | bytes 393224 | tf_op jit(solution)/shard_map/ppermute | solution.py:17
  441.3 16.5 %collective-permute-start = (f32[4,2,1,4096]{3,0,2,1:T(4,128)S(1)}, f32[4,2,1,4096]{3,0,2,1:T(4,128)S(1)}, u32[]{:S(2)}, u32[]{:S(2)}) collective-permute-start(f32[4,2,1,4096]{3,0,2,1:T(4,128)S(1)} %get-tuple-element.110), channel_id=1, source_target_pairs={{1,0},{2,1},{3,2},{4,3},{5,4},{6,5},{7,6},{9,8},{10,9},{11,10},{12... | collective-permute-start | bytes 393224 | tf_op jit(solution)/shard_map/ppermute | solution.py:18
  443.2 14.6 %collective-permute-start.1 = (f32[4,2,1,4096]{3,0,2,1:T(4,128)S(1)}, f32[4,2,1,4096]{3,0,2,1:T(4,128)S(1)}, u32[]{:S(2)}, u32[]{:S(2)}) collective-permute-start(f32[4,2,1,4096]{3,0,2,1:T(4,128)S(1)} %get-tuple-element.109), channel_id=1, source_target_pairs={{0,1},{1,2},{2,3},{3,4},{4,5},{5,6},{6,7},{8,9},{9,10},{10,11},{11... | collective-permute-start | bytes 393224 | tf_op jit(solution)/shard_map/ppermute | solution.py:17
  452.7 13.3 %collective-permute-start.32 = (f32[4,2,1,4096]{3,0,2,1:T(4,128)S(1)}, f32[4,2,1,4096]{3,0,2,1:T(4,128)S(1)}, u32[]{:S(2)}, u32[]{:S(2)}) collective-permute-start(f32[4,2,1,4096]{3,0,2,1:T(4,128)S(1)} %get-tuple-element.46), channel_id=1, source_target_pairs={{1,0},{2,1},{3,2},{4,3},{5,4},{6,5},{7,6},{9,8},{10,9},{11,10},{12... | collective-permute-start | bytes 393224 | tf_op jit(solution)/shard_map/ppermute | solution.py:18
  455.8 10.1 %collective-permute-start.33 = (f32[4,2,1,4096]{3,0,2,1:T(4,128)S(1)}, f32[4,2,1,4096]{3,0,2,1:T(4,128)S(1)}, u32[]{:S(2)}, u32[]{:S(2)}) collective-permute-start(f32[4,2,1,4096]{3,0,2,1:T(4,128)S(1)} %get-tuple-element.45), channel_id=1, source_target_pairs={{0,1},{1,2},{2,3},{3,4},{4,5},{5,6},{6,7},{8,9},{9,10},{10,11},{11... | collective-permute-start | bytes 393224 | tf_op jit(solution)/shard_map/ppermute | solution.py:17
  460.3 13.8 %collective-permute-start.2 = (f32[4,2,1,4096]{3,0,2,1:T(4,128)S(1)}, f32[4,2,1,4096]{3,0,2,1:T(4,128)S(1)}, u32[]{:S(2)}, u32[]{:S(2)}) collective-permute-start(f32[4,2,1,4096]{3,0,2,1:T(4,128)S(1)} %get-tuple-element.106), channel_id=1, source_target_pairs={{1,0},{2,1},{3,2},{4,3},{5,4},{6,5},{7,6},{9,8},{10,9},{11,10},{12... | collective-permute-start | bytes 393224 | tf_op jit(solution)/shard_map/ppermute | solution.py:18
  464.0 10.1 %collective-permute-start.3 = (f32[4,2,1,4096]{3,0,2,1:T(4,128)S(1)}, f32[4,2,1,4096]{3,0,2,1:T(4,128)S(1)}, u32[]{:S(2)}, u32[]{:S(2)}) collective-permute-start(f32[4,2,1,4096]{3,0,2,1:T(4,128)S(1)} %get-tuple-element.105), channel_id=1, source_target_pairs={{0,1},{1,2},{2,3},{3,4},{4,5},{5,6},{6,7},{8,9},{9,10},{10,11},{11... | collective-permute-start | bytes 393224 | tf_op jit(solution)/shard_map/ppermute | solution.py:17
  468.5 13.8 %collective-permute-start.34 = (f32[4,2,1,4096]{3,0,2,1:T(4,128)S(1)}, f32[4,2,1,4096]{3,0,2,1:T(4,128)S(1)}, u32[]{:S(2)}, u32[]{:S(2)}) collective-permute-start(f32[4,2,1,4096]{3,0,2,1:T(4,128)S(1)} %get-tuple-element.42), channel_id=1, source_target_pairs={{1,0},{2,1},{3,2},{4,3},{5,4},{6,5},{7,6},{9,8},{10,9},{11,10},{12... | collective-permute-start | bytes 393224 | tf_op jit(solution)/shard_map/ppermute | solution.py:18
  472.2 10.1 %collective-permute-start.35 = (f32[4,2,1,4096]{3,0,2,1:T(4,128)S(1)}, f32[4,2,1,4096]{3,0,2,1:T(4,128)S(1)}, u32[]{:S(2)}, u32[]{:S(2)}) collective-permute-start(f32[4,2,1,4096]{3,0,2,1:T(4,128)S(1)} %get-tuple-element.41), channel_id=1, source_target_pairs={{0,1},{1,2},{2,3},{3,4},{4,5},{5,6},{6,7},{8,9},{9,10},{10,11},{11... | collective-permute-start | bytes 393224 | tf_op jit(solution)/shard_map/ppermute | solution.py:17
  476.3 13.8 %collective-permute-start.4 = (f32[4,2,1,4096]{3,0,2,1:T(4,128)S(1)}, f32[4,2,1,4096]{3,0,2,1:T(4,128)S(1)}, u32[]{:S(2)}, u32[]{:S(2)}) collective-permute-start(f32[4,2,1,4096]{3,0,2,1:T(4,128)S(1)} %get-tuple-element.102), channel_id=1, source_target_pairs={{1,0},{2,1},{3,2},{4,3},{5,4},{6,5},{7,6},{9,8},{10,9},{11,10},{12... | collective-permute-start | bytes 393224 | tf_op jit(solution)/shard_map/ppermute | solution.py:18
  479.9 10.1 %collective-permute-start.5 = (f32[4,2,1,4096]{3,0,2,1:T(4,128)S(1)}, f32[4,2,1,4096]{3,0,2,1:T(4,128)S(1)}, u32[]{:S(2)}, u32[]{:S(2)}) collective-permute-start(f32[4,2,1,4096]{3,0,2,1:T(4,128)S(1)} %get-tuple-element.101), channel_id=1, source_target_pairs={{0,1},{1,2},{2,3},{3,4},{4,5},{5,6},{6,7},{8,9},{9,10},{10,11},{11... | collective-permute-start | bytes 393224 | tf_op jit(solution)/shard_map/ppermute | solution.py:17
  484.5 13.3 %collective-permute-start.36 = (f32[4,2,1,4096]{3,0,2,1:T(4,128)S(1)}, f32[4,2,1,4096]{3,0,2,1:T(4,128)S(1)}, u32[]{:S(2)}, u32[]{:S(2)}) collective-permute-start(f32[4,2,1,4096]{3,0,2,1:T(4,128)S(1)} %get-tuple-element.38), channel_id=1, source_target_pairs={{1,0},{2,1},{3,2},{4,3},{5,4},{6,5},{7,6},{9,8},{10,9},{11,10},{12... | collective-permute-start | bytes 393224 | tf_op jit(solution)/shard_map/ppermute | solution.py:18
  488.1 9.7 %collective-permute-start.37 = (f32[4,2,1,4096]{3,0,2,1:T(4,128)S(1)}, f32[4,2,1,4096]{3,0,2,1:T(4,128)S(1)}, u32[]{:S(2)}, u32[]{:S(2)}) collective-permute-start(f32[4,2,1,4096]{3,0,2,1:T(4,128)S(1)} %get-tuple-element.37), channel_id=1, source_target_pairs={{0,1},{1,2},{2,3},{3,4},{4,5},{5,6},{6,7},{8,9},{9,10},{10,11},{11... | collective-permute-start | bytes 393224 | tf_op jit(solution)/shard_map/ppermute | solution.py:17
  492.2 13.3 %collective-permute-start.6 = (f32[4,2,1,4096]{3,0,2,1:T(4,128)S(1)}, f32[4,2,1,4096]{3,0,2,1:T(4,128)S(1)}, u32[]{:S(2)}, u32[]{:S(2)}) collective-permute-start(f32[4,2,1,4096]{3,0,2,1:T(4,128)S(1)} %get-tuple-element.98), channel_id=1, source_target_pairs={{1,0},{2,1},{3,2},{4,3},{5,4},{6,5},{7,6},{9,8},{10,9},{11,10},{12... | collective-permute-start | bytes 393224 | tf_op jit(solution)/shard_map/ppermute | solution.py:18
  495.9 9.7 %collective-permute-start.7 = (f32[4,2,1,4096]{3,0,2,1:T(4,128)S(1)}, f32[4,2,1,4096]{3,0,2,1:T(4,128)S(1)}, u32[]{:S(2)}, u32[]{:S(2)}) collective-permute-start(f32[4,2,1,4096]{3,0,2,1:T(4,128)S(1)} %get-tuple-element.97), channel_id=1, source_target_pairs={{0,1},{1,2},{2,3},{3,4},{4,5},{5,6},{6,7},{8,9},{9,10},{10,11},{11... | collective-permute-start | bytes 393224 | tf_op jit(solution)/shard_map/ppermute | solution.py:17
  500.0 14.6 %collective-permute-start.38 = (f32[4,2,1,4096]{3,0,2,1:T(4,128)S(1)}, f32[4,2,1,4096]{3,0,2,1:T(4,128)S(1)}, u32[]{:S(2)}, u32[]{:S(2)}) collective-permute-start(f32[4,2,1,4096]{3,0,2,1:T(4,128)S(1)} %get-tuple-element.34), channel_id=1, source_target_pairs={{1,0},{2,1},{3,2},{4,3},{5,4},{6,5},{7,6},{9,8},{10,9},{11,10},{12... | collective-permute-start | bytes 393224 | tf_op jit(solution)/shard_map/ppermute | solution.py:18
  503.6 11.0 %collective-permute-start.39 = (f32[4,2,1,4096]{3,0,2,1:T(4,128)S(1)}, f32[4,2,1,4096]{3,0,2,1:T(4,128)S(1)}, u32[]{:S(2)}, u32[]{:S(2)}) collective-permute-start(f32[4,2,1,4096]{3,0,2,1:T(4,128)S(1)} %get-tuple-element.33), channel_id=1, source_target_pairs={{0,1},{1,2},{2,3},{3,4},{4,5},{5,6},{6,7},{8,9},{9,10},{10,11},{11... | collective-permute-start | bytes 393224 | tf_op jit(solution)/shard_map/ppermute | solution.py:17
  508.9 14.6 %collective-permute-start.8 = (f32[4,2,1,4096]{3,0,2,1:T(4,128)S(1)}, f32[4,2,1,4096]{3,0,2,1:T(4,128)S(1)}, u32[]{:S(2)}, u32[]{:S(2)}) collective-permute-start(f32[4,2,1,4096]{3,0,2,1:T(4,128)S(1)} %get-tuple-element.94), channel_id=1, source_target_pairs={{1,0},{2,1},{3,2},{4,3},{5,4},{6,5},{7,6},{9,8},{10,9},{11,10},{12... | collective-permute-start | bytes 393224 | tf_op jit(solution)/shard_map/ppermute | solution.py:18
  512.5 11.0 %collective-permute-start.9 = (f32[4,2,1,4096]{3,0,2,1:T(4,128)S(1)}, f32[4,2,1,4096]{3,0,2,1:T(4,128)S(1)}, u32[]{:S(2)}, u32[]{:S(2)}) collective-permute-start(f32[4,2,1,4096]{3,0,2,1:T(4,128)S(1)} %get-tuple-element.93), channel_id=1, source_target_pairs={{0,1},{1,2},{2,3},{3,4},{4,5},{5,6},{6,7},{8,9},{9,10},{10,11},{11... | collective-permute-start | bytes 393224 | tf_op jit(solution)/shard_map/ppermute | solution.py:17
  517.9 14.5 %collective-permute-start.40 = (f32[4,2,1,4096]{3,0,2,1:T(4,128)S(1)}, f32[4,2,1,4096]{3,0,2,1:T(4,128)S(1)}, u32[]{:S(2)}, u32[]{:S(2)}) collective-permute-start(f32[4,2,1,4096]{3,0,2,1:T(4,128)S(1)} %get-tuple-element.30), channel_id=1, source_target_pairs={{1,0},{2,1},{3,2},{4,3},{5,4},{6,5},{7,6},{9,8},{10,9},{11,10},{12... | collective-permute-start | bytes 393224 | tf_op jit(solution)/shard_map/ppermute | solution.py:18
  521.5 10.9 %collective-permute-start.41 = (f32[4,2,1,4096]{3,0,2,1:T(4,128)S(1)}, f32[4,2,1,4096]{3,0,2,1:T(4,128)S(1)}, u32[]{:S(2)}, u32[]{:S(2)}) collective-permute-start(f32[4,2,1,4096]{3,0,2,1:T(4,128)S(1)} %get-tuple-element.29), channel_id=1, source_target_pairs={{0,1},{1,2},{2,3},{3,4},{4,5},{5,6},{6,7},{8,9},{9,10},{10,11},{11... | collective-permute-start | bytes 393224 | tf_op jit(solution)/shard_map/ppermute | solution.py:17
  526.1 14.5 %collective-permute-start.10 = (f32[4,2,1,4096]{3,0,2,1:T(4,128)S(1)}, f32[4,2,1,4096]{3,0,2,1:T(4,128)S(1)}, u32[]{:S(2)}, u32[]{:S(2)}) collective-permute-start(f32[4,2,1,4096]{3,0,2,1:T(4,128)S(1)} %get-tuple-element.90), channel_id=1, source_target_pairs={{1,0},{2,1},{3,2},{4,3},{5,4},{6,5},{7,6},{9,8},{10,9},{11,10},{12... | collective-permute-start | bytes 393224 | tf_op jit(solution)/shard_map/ppermute | solution.py:18
  529.7 10.9 %collective-permute-start.11 = (f32[4,2,1,4096]{3,0,2,1:T(4,128)S(1)}, f32[4,2,1,4096]{3,0,2,1:T(4,128)S(1)}, u32[]{:S(2)}, u32[]{:S(2)}) collective-permute-start(f32[4,2,1,4096]{3,0,2,1:T(4,128)S(1)} %get-tuple-element.89), channel_id=1, source_target_pairs={{0,1},{1,2},{2,3},{3,4},{4,5},{5,6},{6,7},{8,9},{9,10},{10,11},{11... | collective-permute-start | bytes 393224 | tf_op jit(solution)/shard_map/ppermute | solution.py:17
  535.0 13.6 %collective-permute-start.42 = (f32[4,2,1,4096]{3,0,2,1:T(4,128)S(1)}, f32[4,2,1,4096]{3,0,2,1:T(4,128)S(1)}, u32[]{:S(2)}, u32[]{:S(2)}) collective-permute-start(f32[4,2,1,4096]{3,0,2,1:T(4,128)S(1)} %get-tuple-element.26), channel_id=1, source_target_pairs={{1,0},{2,1},{3,2},{4,3},{5,4},{6,5},{7,6},{9,8},{10,9},{11,10},{12... | collective-permute-start | bytes 393224 | tf_op jit(solution)/shard_map/ppermute | solution.py:18
  538.6 9.9 %collective-permute-start.43 = (f32[4,2,1,4096]{3,0,2,1:T(4,128)S(1)}, f32[4,2,1,4096]{3,0,2,1:T(4,128)S(1)}, u32[]{:S(2)}, u32[]{:S(2)}) collective-permute-start(f32[4,2,1,4096]{3,0,2,1:T(4,128)S(1)} %get-tuple-element.25), channel_id=1, source_target_pairs={{0,1},{1,2},{2,3},{3,4},{4,5},{5,6},{6,7},{8,9},{9,10},{10,11},{11... | collective-permute-start | bytes 393224 | tf_op jit(solution)/shard_map/ppermute | solution.py:17
  542.7 13.6 %collective-permute-start.12 = (f32[4,2,1,4096]{3,0,2,1:T(4,128)S(1)}, f32[4,2,1,4096]{3,0,2,1:T(4,128)S(1)}, u32[]{:S(2)}, u32[]{:S(2)}) collective-permute-start(f32[4,2,1,4096]{3,0,2,1:T(4,128)S(1)} %get-tuple-element.86), channel_id=1, source_target_pairs={{1,0},{2,1},{3,2},{4,3},{5,4},{6,5},{7,6},{9,8},{10,9},{11,10},{12... | collective-permute-start | bytes 393224 | tf_op jit(solution)/shard_map/ppermute | solution.py:18
  546.4 9.9 %collective-permute-start.13 = (f32[4,2,1,4096]{3,0,2,1:T(4,128)S(1)}, f32[4,2,1,4096]{3,0,2,1:T(4,128)S(1)}, u32[]{:S(2)}, u32[]{:S(2)}) collective-permute-start(f32[4,2,1,4096]{3,0,2,1:T(4,128)S(1)} %get-tuple-element.85), channel_id=1, source_target_pairs={{0,1},{1,2},{2,3},{3,4},{4,5},{5,6},{6,7},{8,9},{9,10},{10,11},{11... | collective-permute-start | bytes 393224 | tf_op jit(solution)/shard_map/ppermute | solution.py:17
  550.7 13.3 %collective-permute-start.44 = (f32[4,2,1,4096]{3,0,2,1:T(4,128)S(1)}, f32[4,2,1,4096]{3,0,2,1:T(4,128)S(1)}, u32[]{:S(2)}, u32[]{:S(2)}) collective-permute-start(f32[4,2,1,4096]{3,0,2,1:T(4,128)S(1)} %get-tuple-element.22), channel_id=1, source_target_pairs={{1,0},{2,1},{3,2},{4,3},{5,4},{6,5},{7,6},{9,8},{10,9},{11,10},{12... | collective-permute-start | bytes 393224 | tf_op jit(solution)/shard_map/ppermute | solution.py:18
  554.4 9.7 %collective-permute-start.45 = (f32[4,2,1,4096]{3,0,2,1:T(4,128)S(1)}, f32[4,2,1,4096]{3,0,2,1:T(4,128)S(1)}, u32[]{:S(2)}, u32[]{:S(2)}) collective-permute-start(f32[4,2,1,4096]{3,0,2,1:T(4,128)S(1)} %get-tuple-element.21), channel_id=1, source_target_pairs={{0,1},{1,2},{2,3},{3,4},{4,5},{5,6},{6,7},{8,9},{9,10},{10,11},{11... | collective-permute-start | bytes 393224 | tf_op jit(solution)/shard_map/ppermute | solution.py:17
  558.5 13.3 %collective-permute-start.14 = (f32[4,2,1,4096]{3,0,2,1:T(4,128)S(1)}, f32[4,2,1,4096]{3,0,2,1:T(4,128)S(1)}, u32[]{:S(2)}, u32[]{:S(2)}) collective-permute-start(f32[4,2,1,4096]{3,0,2,1:T(4,128)S(1)} %get-tuple-element.82), channel_id=1, source_target_pairs={{1,0},{2,1},{3,2},{4,3},{5,4},{6,5},{7,6},{9,8},{10,9},{11,10},{12... | collective-permute-start | bytes 393224 | tf_op jit(solution)/shard_map/ppermute | solution.py:18
  562.1 9.7 %collective-permute-start.15 = (f32[4,2,1,4096]{3,0,2,1:T(4,128)S(1)}, f32[4,2,1,4096]{3,0,2,1:T(4,128)S(1)}, u32[]{:S(2)}, u32[]{:S(2)}) collective-permute-start(f32[4,2,1,4096]{3,0,2,1:T(4,128)S(1)} %get-tuple-element.81), channel_id=1, source_target_pairs={{0,1},{1,2},{2,3},{3,4},{4,5},{5,6},{6,7},{8,9},{9,10},{10,11},{11... | collective-permute-start | bytes 393224 | tf_op jit(solution)/shard_map/ppermute | solution.py:17
  566.2 15.5 %collective-permute-start.46 = (f32[4,2,1,4096]{3,0,2,1:T(4,128)S(1)}, f32[4,2,1,4096]{3,0,2,1:T(4,128)S(1)}, u32[]{:S(2)}, u32[]{:S(2)}) collective-permute-start(f32[4,2,1,4096]{3,0,2,1:T(4,128)S(1)} %get-tuple-element.18), channel_id=1, source_target_pairs={{1,0},{2,1},{3,2},{4,3},{5,4},{6,5},{7,6},{9,8},{10,9},{11,10},{12... | collective-permute-start | bytes 393224 | tf_op jit(solution)/shard_map/ppermute | solution.py:18
  569.9 11.8 %collective-permute-start.47 = (f32[4,2,1,4096]{3,0,2,1:T(4,128)S(1)}, f32[4,2,1,4096]{3,0,2,1:T(4,128)S(1)}, u32[]{:S(2)}, u32[]{:S(2)}) collective-permute-start(f32[4,2,1,4096]{3,0,2,1:T(4,128)S(1)} %get-tuple-element.17), channel_id=1, source_target_pairs={{0,1},{1,2},{2,3},{3,4},{4,5},{5,6},{6,7},{8,9},{9,10},{10,11},{11... | collective-permute-start | bytes 393224 | tf_op jit(solution)/shard_map/ppermute | solution.py:17
  575.1 14.2 %collective-permute-start.16 = (f32[4,2,1,4096]{3,0,2,1:T(4,128)S(1)}, f32[4,2,1,4096]{3,0,2,1:T(4,128)S(1)}, u32[]{:S(2)}, u32[]{:S(2)}) collective-permute-start(f32[4,2,1,4096]{3,0,2,1:T(4,128)S(1)} %get-tuple-element.78), channel_id=1, source_target_pairs={{1,0},{2,1},{3,2},{4,3},{5,4},{6,5},{7,6},{9,8},{10,9},{11,10},{12... | collective-permute-start | bytes 393224 | tf_op jit(solution)/shard_map/ppermute | solution.py:18
  578.8 10.5 %collective-permute-start.17 = (f32[4,2,1,4096]{3,0,2,1:T(4,128)S(1)}, f32[4,2,1,4096]{3,0,2,1:T(4,128)S(1)}, u32[]{:S(2)}, u32[]{:S(2)}) collective-permute-start(f32[4,2,1,4096]{3,0,2,1:T(4,128)S(1)} %get-tuple-element.77), channel_id=1, source_target_pairs={{0,1},{1,2},{2,3},{3,4},{4,5},{5,6},{6,7},{8,9},{9,10},{10,11},{11... | collective-permute-start | bytes 393224 | tf_op jit(solution)/shard_map/ppermute | solution.py:17
  592.6 8.5 %collective-permute-start.18 = (f32[4,2,1,4096]{3,0,2,1:T(4,128)}, f32[4,2,1,4096]{3,0,2,1:T(4,128)S(1)}, u32[]{:S(2)}, u32[]{:S(2)}) collective-permute-start(f32[4,2,1,4096]{3,0,2,1:T(4,128)} %get-tuple-element.74), channel_id=1, source_target_pairs={{1,0},{2,1},{3,2},{4,3},{5,4},{6,5},{7,6},{9,8},{10,9},{11,10},{12... | collective-permute-start | bytes 393224 | tf_op jit(solution)/shard_map/ppermute | solution.py:18
  596.2 6.3 collective-permute-start.19
  607.0 7.0 collective-permute-start.21
  618.1 9.0 %collective-permute-start.23 = (f32[4,2,1,4096]{3,0,2,1:T(4,128)S(1)}, f32[4,2,1,4096]{3,0,2,1:T(4,128)S(1)}, u32[]{:S(2)}, u32[]{:S(2)}) collective-permute-start(f32[4,2,1,4096]{3,0,2,1:T(4,128)S(1)} %get-tuple-element.65), channel_id=1, source_target_pairs={{0,1},{1,2},{2,3},{3,4},{4,5},{5,6},{6,7},{8,9},{9,10},{10,11},{11... | collective-permute-start | bytes 393224 | tf_op jit(solution)/shard_map/ppermute | solution.py:17
  (16 other events, 62.0 us)
Sparse Core Ops, SparseCore 0:
  16.9 418.6 all-reduce.26
  601.2 236.1 reduce-scatter.1
where the time goes:
time: 854 us; the launch traced here: 845 us
  waiting for transfers between devices  612 us (72%)
  starting transfers between devices  126 us (15%)
  other arithmetic  78.6 us (9%)
  between operations  18.1 us (2%)
  local copies, waits for them, and re-layouts  9.5 us (1%)
    psum x1, waiting for transfers between devices, broadcast(): return lax.psum(block, axis)  387 us
    reduce_scatter x1, waiting for transfers between devices, body(): lax.psum_scatter(buffer, 'illum', scatter_dimension=0, tiled=True)  206 us
    ppermute x24, starting transfers between devices, extended(): after = lax.ppermute(initial, axis, down)  76 us
    ppermute x24, starting transfers between devices, extended(): before = lax.ppermute(last, axis, up)  50.3 us
    ppermute x24, waiting for transfers between devices, extended(): before = lax.ppermute(last, axis, up)  18.5 us
    concatenate x24, other arithmetic, extended(): array = jnp.concatenate([before, array, after], axis=dim)  18.3 us
    sub x24, other arithmetic, laplace_padded(): framed[:, :, 2:, 1:-1] + framed[:, :, :-2, 1:-1]  17.8 us
  transfers between devices with their start and end apart: 50, of which 10 were waited for; matrix products, arithmetic and copies ran while one was open for 10% of the time, Pallas kernels for 0%

commit v1 on v0

--- a/solution.py
+++ b/solution.py
@@ -22,7 +22,7 @@
 
 def broadcast(block, axis, holder):
     block = jnp.where(lax.axis_index(axis) == holder, block, jnp.zeros_like(block))
-    return lax.psum(block, axis)
+    return jnp.sum(lax.all_gather(block, axis), axis=0)
 
 
 def laplace_padded(padded):

time: 854 us -> 758 us (0.89)
  waiting for transfers between devices: 612 us -> 497 us
  starting transfers between devices: 126 us -> 138 us
  other arithmetic: 78.6 us -> 87.5 us
    psum x1 -> x0, waiting for transfers between devices: 387 us -> none  [broadcast(): return lax.psum(block, axis)]
    all_gather x0 -> x3, waiting for transfers between devices: none -> 275 us  [broadcast(): return jnp.sum(lax.all_gather(block, axis), axis=0)]
    ppermute x24, waiting for transfers between devices: 0.86 us -> 10.8 us  [extended(): after = lax.ppermute(initial, axis, down)]
    ppermute x24, waiting for transfers between devices: 18.5 us -> 8.9 us  [extended(): before = lax.ppermute(last, axis, up)]
  transfers between devices with their start and end apart: 50 -> 52, of which waited for: 10 -> 16; matrix products, arithmetic and copies ran while one was open for 10% -> 10% of each run, Pallas kernels for 0% -> 0%
where the time goes in v1:
time: 758 us; the launch traced here: 748 us
  waiting for transfers between devices  497 us (66%)
  starting transfers between devices  138 us (18%)
  other arithmetic  87.5 us (12%)
  between operations  17.4 us (2%)
  local copies, waits for them, and re-layouts  8.05 us (1%)
    all_gather x3, waiting for transfers between devices, broadcast(): return jnp.sum(lax.all_gather(block, axis), axis=0)  275 us
    reduce_scatter x1, waiting for transfers between devices, body(): lax.psum_scatter(buffer, 'illum', scatter_dimension=0, tiled=True)  202 us
    ppermute x24, starting transfers between devices, extended(): after = lax.ppermute(initial, axis, down)  80.9 us
    ppermute x24, starting transfers between devices, extended(): before = lax.ppermute(last, axis, up)  56.5 us
    concatenate x24, other arithmetic, extended(): array = jnp.concatenate([before, array, after], axis=dim)  18.3 us
    sub x24, other arithmetic, laplace_padded(): framed[:, :, 2:, 1:-1] + framed[:, :, :-2, 1:-1]  17.9 us
  transfers between devices with their start and end apart: 52, of which 16 were waited for; matrix products, arithmetic and copies ran while one was open for 10% of the time, Pallas kernels for 0%

profile of v1, /device:TPU:32, one launch (start us, length us, event | category | flops | bytes accessed | tf_op | source)
XLA Modules:
  0.0 747.7 jit_solution(12589497268074697797)
XLA Ops:
  15.0 1.9 collective-permute-start.25
  16.9 3.6 collective-permute-start.24
  27.3 4.1 collective-permute-start.27
  38.8 4.4 collective-permute-start.29
  45.2 2.4 collective-permute-done.28
  50.2 3.8 collective-permute-start.31
  54.0 2.2 collective-permute-start.30
  63.4 63.3 %all-gather.8.cloned.1.call-done = f32[32,8,4096]{2,1,0:T(8,128)} async-done(((f32[1,8,4096]{2,1,0:T(8,128)}), f32[32,8,4096]{2,1,0:T(8,128)}) %all-gather.8.cloned.1.call-update) | async-done | bytes 4194320 | tf_op jit(solution)/shard_map/all_gather | solution.py:25
  126.7 2.4 reduce_sum.56
  129.1 106.6 %all-gather.6.cloned.1.call-done = f32[32,8,4096]{2,1,0:T(8,128)} async-done(((f32[1,8,4096]{2,1,0:T(8,128)}), f32[32,8,4096]{2,1,0:T(8,128)}) %all-gather.6.cloned.1.call-update) | async-done | bytes 4194320 | tf_op jit(solution)/shard_map/all_gather | solution.py:25
  235.7 2.4 reduce_sum.55
  239.5 105.2 %all-gather.4.cloned.1.call-done = f32[32,8,4096]{2,1,0:T(8,128)} async-done(((f32[1,8,4096]{2,1,0:T(8,128)}), f32[32,8,4096]{2,1,0:T(8,128)}) %all-gather.4.cloned.1.call-update) | async-done | bytes 4194320 | tf_op jit(solution)/shard_map/all_gather | solution.py:25
  344.7 2.4 reduce_sum.54
  348.0 4.2 fusion.105
  352.3 1.9 collective-permute-start.1
  354.2 3.6 collective-permute-start
  360.2 3.6 collective-permute-start.32
  368.4 4.2 collective-permute-start.2
  377.1 3.6 collective-permute-start.34
  384.9 3.6 collective-permute-start.4
  390.8 1.9 collective-permute-start.37
  392.7 3.6 collective-permute-start.36
  400.6 3.6 collective-permute-start.6
  406.4 1.9 collective-permute-start.39
  408.4 3.8 collective-permute-start.38
  419.4 2.7 collective-permute-start.41
  422.2 3.0 collective-permute-start.40
  427.2 3.6 collective-permute-start.8
  436.0 2.7 collective-permute-start.11
  438.7 3.0 collective-permute-start.10
  444.3 1.9 collective-permute-start.43
  446.3 3.9 collective-permute-start.42
  454.3 3.6 collective-permute-start.12
  460.2 1.9 collective-permute-start.45
  462.1 3.6 collective-permute-start.44
  469.9 3.6 collective-permute-start.14
  475.8 1.9 collective-permute-start.47
  477.7 3.6 collective-permute-start.46
  486.6 4.0 collective-permute-start.16
  494.2 4.7 fusion.117
  504.1 3.6 collective-permute-start.18
  507.7 2.9 multiply_add_fusion
  512.9 2.3 collective-permute-start.21
  515.2 3.3 collective-permute-start.20
  523.9 4.0 collective-permute-start.23
  527.9 2.3 collective-permute-start.22
  530.2 4.5 collective-permute-done.23
  539.2 201.8 %reduce-scatter.2.cloned.1.call-done = f32[1,8,4096]{2,1,0:T(8,128)} async-done(((f32[32,8,4096]{2,1,0:T(8,128)}), f32[1,8,4096]{2,1,0:T(8,128)}) %reduce-scatter.2.cloned.1.call-update) | async-done | bytes 131088 | tf_op jit(solution)/shard_map/reduce_scatter | solution.py:112
  (208 shorter events, 113.2 us)
Async XLA Ops:
  7.2 119.6 %all-gather.8.cloned.1.call-start = ((), (), s32[]{:S(2)}) async-start(), calls=%async_computation.3 | async-start | bytes 4325376 | tf_op jit(solution)/shard_map/all_gather | solution.py:25
  12.2 223.5 %all-gather.6.cloned.1.call-start = ((), (), s32[]{:S(2)}) async-start(), calls=%async_computation.2 | async-start | bytes 4325376 | tf_op jit(solution)/shard_map/all_gather | solution.py:25
  13.0 331.7 %all-gather.4.cloned.1.call-start = ((), (), s32[]{:S(2)}) async-start(), calls=%async_computation.1 | async-start | bytes 4325376 | tf_op jit(solution)/shard_map/all_gather | solution.py:25
  15.0 6.3 collective-permute-start.25
  20.6 720.4 %reduce-scatter.2.cloned.1.call-start = ((), (), s32[]{:S(2)}) async-start(), calls=%async_computation.4 | async-start | bytes 4325376 | tf_op jit(solution)/shard_map/reduce_scatter | solution.py:112
  27.3 7.6 %collective-permute-start.27 = (f32[4,2,1,4096]{3,0,2,1:T(4,128)}, f32[4,2,1,4096]{3,0,2,1:T(4,128)S(1)}, u32[]{:S(2)}, u32[]{:S(2)}) collective-permute-start(f32[4,2,1,4096]{3,0,2,1:T(4,128)} %get-tuple-element.54), channel_id=1, source_target_pairs={{0,1},{1,2},{2,3},{3,4},{4,5},{5,6},{6,7},{8,9},{9,10},{10,11},{11... | collective-permute-start | bytes 393224 | tf_op jit(solution)/shard_map/ppermute | solution.py:17
  38.8 6.4 collective-permute-start.29
  50.2 8.6 %collective-permute-start.31 = (f32[4,2,1,4096]{3,0,2,1:T(4,128)S(1)}, f32[4,2,1,4096]{3,0,2,1:T(4,128)S(1)}, u32[]{:S(2)}, u32[]{:S(2)}) collective-permute-start(f32[4,2,1,4096]{3,0,2,1:T(4,128)S(1)} %get-tuple-element.46), channel_id=1, source_target_pairs={{0,1},{1,2},{2,3},{3,4},{4,5},{5,6},{6,7},{8,9},{9,10},{10,11},{11... | collective-permute-start | bytes 393224 | tf_op jit(solution)/shard_map/ppermute | solution.py:17
  54.0 6.2 collective-permute-start.30
  352.3 11.5 %collective-permute-start.1 = (f32[4,2,1,4096]{3,0,2,1:T(4,128)S(1)}, f32[4,2,1,4096]{3,0,2,1:T(4,128)S(1)}, u32[]{:S(2)}, u32[]{:S(2)}) collective-permute-start(f32[4,2,1,4096]{3,0,2,1:T(4,128)S(1)} %get-tuple-element.106), channel_id=1, source_target_pairs={{0,1},{1,2},{2,3},{3,4},{4,5},{5,6},{6,7},{8,9},{9,10},{10,11},{11... | collective-permute-start | bytes 393224 | tf_op jit(solution)/shard_map/ppermute | solution.py:17
  354.2 9.6 %collective-permute-start = (f32[4,2,1,4096]{3,0,2,1:T(4,128)S(1)}, f32[4,2,1,4096]{3,0,2,1:T(4,128)S(1)}, u32[]{:S(2)}, u32[]{:S(2)}) collective-permute-start(f32[4,2,1,4096]{3,0,2,1:T(4,128)S(1)} %get-tuple-element.107), channel_id=1, source_target_pairs={{1,0},{2,1},{3,2},{4,3},{5,4},{6,5},{7,6},{9,8},{10,9},{11,10},{12... | collective-permute-start | bytes 393224 | tf_op jit(solution)/shard_map/ppermute | solution.py:18
  358.2 14.3 %collective-permute-start.33 = (f32[4,2,1,4096]{3,0,2,1:T(4,128)S(1)}, f32[4,2,1,4096]{3,0,2,1:T(4,128)S(1)}, u32[]{:S(2)}, u32[]{:S(2)}) collective-permute-start(f32[4,2,1,4096]{3,0,2,1:T(4,128)S(1)} %get-tuple-element.42), channel_id=1, source_target_pairs={{0,1},{1,2},{2,3},{3,4},{4,5},{5,6},{6,7},{8,9},{9,10},{10,11},{11... | collective-permute-start | bytes 393224 | tf_op jit(solution)/shard_map/ppermute | solution.py:17
  360.2 12.4 %collective-permute-start.32 = (f32[4,2,1,4096]{3,0,2,1:T(4,128)S(1)}, f32[4,2,1,4096]{3,0,2,1:T(4,128)S(1)}, u32[]{:S(2)}, u32[]{:S(2)}) collective-permute-start(f32[4,2,1,4096]{3,0,2,1:T(4,128)S(1)} %get-tuple-element.43), channel_id=1, source_target_pairs={{1,0},{2,1},{3,2},{4,3},{5,4},{6,5},{7,6},{9,8},{10,9},{11,10},{12... | collective-permute-start | bytes 393224 | tf_op jit(solution)/shard_map/ppermute | solution.py:18
  366.4 14.3 %collective-permute-start.3 = (f32[4,2,1,4096]{3,0,2,1:T(4,128)S(1)}, f32[4,2,1,4096]{3,0,2,1:T(4,128)S(1)}, u32[]{:S(2)}, u32[]{:S(2)}) collective-permute-start(f32[4,2,1,4096]{3,0,2,1:T(4,128)S(1)} %get-tuple-element.102), channel_id=1, source_target_pairs={{0,1},{1,2},{2,3},{3,4},{4,5},{5,6},{6,7},{8,9},{9,10},{10,11},{11... | collective-permute-start | bytes 393224 | tf_op jit(solution)/shard_map/ppermute | solution.py:17
  368.4 12.4 %collective-permute-start.2 = (f32[4,2,1,4096]{3,0,2,1:T(4,128)S(1)}, f32[4,2,1,4096]{3,0,2,1:T(4,128)S(1)}, u32[]{:S(2)}, u32[]{:S(2)}) collective-permute-start(f32[4,2,1,4096]{3,0,2,1:T(4,128)S(1)} %get-tuple-element.103), channel_id=1, source_target_pairs={{1,0},{2,1},{3,2},{4,3},{5,4},{6,5},{7,6},{9,8},{10,9},{11,10},{12... | collective-permute-start | bytes 393224 | tf_op jit(solution)/shard_map/ppermute | solution.py:18
  375.2 13.4 %collective-permute-start.35 = (f32[4,2,1,4096]{3,0,2,1:T(4,128)S(1)}, f32[4,2,1,4096]{3,0,2,1:T(4,128)S(1)}, u32[]{:S(2)}, u32[]{:S(2)}) collective-permute-start(f32[4,2,1,4096]{3,0,2,1:T(4,128)S(1)} %get-tuple-element.38), channel_id=1, source_target_pairs={{0,1},{1,2},{2,3},{3,4},{4,5},{5,6},{6,7},{8,9},{9,10},{10,11},{11... | collective-permute-start | bytes 393224 | tf_op jit(solution)/shard_map/ppermute | solution.py:17
  377.1 11.5 %collective-permute-start.34 = (f32[4,2,1,4096]{3,0,2,1:T(4,128)S(1)}, f32[4,2,1,4096]{3,0,2,1:T(4,128)S(1)}, u32[]{:S(2)}, u32[]{:S(2)}) collective-permute-start(f32[4,2,1,4096]{3,0,2,1:T(4,128)S(1)} %get-tuple-element.39), channel_id=1, source_target_pairs={{1,0},{2,1},{3,2},{4,3},{5,4},{6,5},{7,6},{9,8},{10,9},{11,10},{12... | collective-permute-start | bytes 393224 | tf_op jit(solution)/shard_map/ppermute | solution.py:18
  383.0 13.4 %collective-permute-start.5 = (f32[4,2,1,4096]{3,0,2,1:T(4,128)S(1)}, f32[4,2,1,4096]{3,0,2,1:T(4,128)S(1)}, u32[]{:S(2)}, u32[]{:S(2)}) collective-permute-start(f32[4,2,1,4096]{3,0,2,1:T(4,128)S(1)} %get-tuple-element.98), channel_id=1, source_target_pairs={{0,1},{1,2},{2,3},{3,4},{4,5},{5,6},{6,7},{8,9},{9,10},{10,11},{11... | collective-permute-start | bytes 393224 | tf_op jit(solution)/shard_map/ppermute | solution.py:17
  384.9 11.5 %collective-permute-start.4 = (f32[4,2,1,4096]{3,0,2,1:T(4,128)S(1)}, f32[4,2,1,4096]{3,0,2,1:T(4,128)S(1)}, u32[]{:S(2)}, u32[]{:S(2)}) collective-permute-start(f32[4,2,1,4096]{3,0,2,1:T(4,128)S(1)} %get-tuple-element.99), channel_id=1, source_target_pairs={{1,0},{2,1},{3,2},{4,3},{5,4},{6,5},{7,6},{9,8},{10,9},{11,10},{12... | collective-permute-start | bytes 393224 | tf_op jit(solution)/shard_map/ppermute | solution.py:18
  390.8 13.4 %collective-permute-start.37 = (f32[4,2,1,4096]{3,0,2,1:T(4,128)S(1)}, f32[4,2,1,4096]{3,0,2,1:T(4,128)S(1)}, u32[]{:S(2)}, u32[]{:S(2)}) collective-permute-start(f32[4,2,1,4096]{3,0,2,1:T(4,128)S(1)} %get-tuple-element.34), channel_id=1, source_target_pairs={{0,1},{1,2},{2,3},{3,4},{4,5},{5,6},{6,7},{8,9},{9,10},{10,11},{11... | collective-permute-start | bytes 393224 | tf_op jit(solution)/shard_map/ppermute | solution.py:17
  392.7 11.5 %collective-permute-start.36 = (f32[4,2,1,4096]{3,0,2,1:T(4,128)S(1)}, f32[4,2,1,4096]{3,0,2,1:T(4,128)S(1)}, u32[]{:S(2)}, u32[]{:S(2)}) collective-permute-start(f32[4,2,1,4096]{3,0,2,1:T(4,128)S(1)} %get-tuple-element.35), channel_id=1, source_target_pairs={{1,0},{2,1},{3,2},{4,3},{5,4},{6,5},{7,6},{9,8},{10,9},{11,10},{12... | collective-permute-start | bytes 393224 | tf_op jit(solution)/shard_map/ppermute | solution.py:18
  398.6 13.6 %collective-permute-start.7 = (f32[4,2,1,4096]{3,0,2,1:T(4,128)S(1)}, f32[4,2,1,4096]{3,0,2,1:T(4,128)S(1)}, u32[]{:S(2)}, u32[]{:S(2)}) collective-permute-start(f32[4,2,1,4096]{3,0,2,1:T(4,128)S(1)} %get-tuple-element.94), channel_id=1, source_target_pairs={{0,1},{1,2},{2,3},{3,4},{4,5},{5,6},{6,7},{8,9},{9,10},{10,11},{11... | collective-permute-start | bytes 393224 | tf_op jit(solution)/shard_map/ppermute | solution.py:17
  400.6 11.7 %collective-permute-start.6 = (f32[4,2,1,4096]{3,0,2,1:T(4,128)S(1)}, f32[4,2,1,4096]{3,0,2,1:T(4,128)S(1)}, u32[]{:S(2)}, u32[]{:S(2)}) collective-permute-start(f32[4,2,1,4096]{3,0,2,1:T(4,128)S(1)} %get-tuple-element.95), channel_id=1, source_target_pairs={{1,0},{2,1},{3,2},{4,3},{5,4},{6,5},{7,6},{9,8},{10,9},{11,10},{12... | collective-permute-start | bytes 393224 | tf_op jit(solution)/shard_map/ppermute | solution.py:18
  406.4 7.5 %collective-permute-start.39 = (f32[4,2,1,4096]{3,0,2,1:T(4,128)S(1)}, f32[4,2,1,4096]{3,0,2,1:T(4,128)S(1)}, u32[]{:S(2)}, u32[]{:S(2)}) collective-permute-start(f32[4,2,1,4096]{3,0,2,1:T(4,128)S(1)} %get-tuple-element.30), channel_id=1, source_target_pairs={{0,1},{1,2},{2,3},{3,4},{4,5},{5,6},{6,7},{8,9},{9,10},{10,11},{11... | collective-permute-start | bytes 393224 | tf_op jit(solution)/shard_map/ppermute | solution.py:17
  408.4 6.1 collective-permute-start.38
  419.4 22.2 %collective-permute-start.41 = (f32[4,2,1,4096]{3,0,2,1:T(4,128)S(1)}, f32[4,2,1,4096]{3,0,2,1:T(4,128)S(1)}, u32[]{:S(2)}, u32[]{:S(2)}) collective-permute-start(f32[4,2,1,4096]{3,0,2,1:T(4,128)S(1)} %get-tuple-element.26), channel_id=1, source_target_pairs={{0,1},{1,2},{2,3},{3,4},{4,5},{5,6},{6,7},{8,9},{9,10},{10,11},{11... | collective-permute-start | bytes 393224 | tf_op jit(solution)/shard_map/ppermute | solution.py:17
  422.2 19.5 %collective-permute-start.40 = (f32[4,2,1,4096]{3,0,2,1:T(4,128)S(1)}, f32[4,2,1,4096]{3,0,2,1:T(4,128)S(1)}, u32[]{:S(2)}, u32[]{:S(2)}) collective-permute-start(f32[4,2,1,4096]{3,0,2,1:T(4,128)S(1)} %get-tuple-element.27), channel_id=1, source_target_pairs={{1,0},{2,1},{3,2},{4,3},{5,4},{6,5},{7,6},{9,8},{10,9},{11,10},{12... | collective-permute-start | bytes 393224 | tf_op jit(solution)/shard_map/ppermute | solution.py:18
  425.2 6.3 collective-permute-start.9
  436.0 14.2 %collective-permute-start.11 = (f32[4,2,1,4096]{3,0,2,1:T(4,128)S(1)}, f32[4,2,1,4096]{3,0,2,1:T(4,128)S(1)}, u32[]{:S(2)}, u32[]{:S(2)}) collective-permute-start(f32[4,2,1,4096]{3,0,2,1:T(4,128)S(1)} %get-tuple-element.86), channel_id=1, source_target_pairs={{0,1},{1,2},{2,3},{3,4},{4,5},{5,6},{6,7},{8,9},{9,10},{10,11},{11... | collective-permute-start | bytes 393224 | tf_op jit(solution)/shard_map/ppermute | solution.py:17
  438.7 11.5 %collective-permute-start.10 = (f32[4,2,1,4096]{3,0,2,1:T(4,128)S(1)}, f32[4,2,1,4096]{3,0,2,1:T(4,128)S(1)}, u32[]{:S(2)}, u32[]{:S(2)}) collective-permute-start(f32[4,2,1,4096]{3,0,2,1:T(4,128)S(1)} %get-tuple-element.87), channel_id=1, source_target_pairs={{1,0},{2,1},{3,2},{4,3},{5,4},{6,5},{7,6},{9,8},{10,9},{11,10},{12... | collective-permute-start | bytes 393224 | tf_op jit(solution)/shard_map/ppermute | solution.py:18
  444.3 13.6 %collective-permute-start.43 = (f32[4,2,1,4096]{3,0,2,1:T(4,128)S(1)}, f32[4,2,1,4096]{3,0,2,1:T(4,128)S(1)}, u32[]{:S(2)}, u32[]{:S(2)}) collective-permute-start(f32[4,2,1,4096]{3,0,2,1:T(4,128)S(1)} %get-tuple-element.22), channel_id=1, source_target_pairs={{0,1},{1,2},{2,3},{3,4},{4,5},{5,6},{6,7},{8,9},{9,10},{10,11},{11... | collective-permute-start | bytes 393224 | tf_op jit(solution)/shard_map/ppermute | solution.py:17
  446.3 11.7 %collective-permute-start.42 = (f32[4,2,1,4096]{3,0,2,1:T(4,128)S(1)}, f32[4,2,1,4096]{3,0,2,1:T(4,128)S(1)}, u32[]{:S(2)}, u32[]{:S(2)}) collective-permute-start(f32[4,2,1,4096]{3,0,2,1:T(4,128)S(1)} %get-tuple-element.23), channel_id=1, source_target_pairs={{1,0},{2,1},{3,2},{4,3},{5,4},{6,5},{7,6},{9,8},{10,9},{11,10},{12... | collective-permute-start | bytes 393224 | tf_op jit(solution)/shard_map/ppermute | solution.py:18
  452.4 13.4 %collective-permute-start.13 = (f32[4,2,1,4096]{3,0,2,1:T(4,128)S(1)}, f32[4,2,1,4096]{3,0,2,1:T(4,128)S(1)}, u32[]{:S(2)}, u32[]{:S(2)}) collective-permute-start(f32[4,2,1,4096]{3,0,2,1:T(4,128)S(1)} %get-tuple-element.82), channel_id=1, source_target_pairs={{0,1},{1,2},{2,3},{3,4},{4,5},{5,6},{6,7},{8,9},{9,10},{10,11},{11... | collective-permute-start | bytes 393224 | tf_op jit(solution)/shard_map/ppermute | solution.py:17
  454.3 11.5 %collective-permute-start.12 = (f32[4,2,1,4096]{3,0,2,1:T(4,128)S(1)}, f32[4,2,1,4096]{3,0,2,1:T(4,128)S(1)}, u32[]{:S(2)}, u32[]{:S(2)}) collective-permute-start(f32[4,2,1,4096]{3,0,2,1:T(4,128)S(1)} %get-tuple-element.83), channel_id=1, source_target_pairs={{1,0},{2,1},{3,2},{4,3},{5,4},{6,5},{7,6},{9,8},{10,9},{11,10},{12... | collective-permute-start | bytes 393224 | tf_op jit(solution)/shard_map/ppermute | solution.py:18
  460.2 13.4 %collective-permute-start.45 = (f32[4,2,1,4096]{3,0,2,1:T(4,128)S(1)}, f32[4,2,1,4096]{3,0,2,1:T(4,128)S(1)}, u32[]{:S(2)}, u32[]{:S(2)}) collective-permute-start(f32[4,2,1,4096]{3,0,2,1:T(4,128)S(1)} %get-tuple-element.18), channel_id=1, source_target_pairs={{0,1},{1,2},{2,3},{3,4},{4,5},{5,6},{6,7},{8,9},{9,10},{10,11},{11... | collective-permute-start | bytes 393224 | tf_op jit(solution)/shard_map/ppermute | solution.py:17
  462.1 11.5 %collective-permute-start.44 = (f32[4,2,1,4096]{3,0,2,1:T(4,128)S(1)}, f32[4,2,1,4096]{3,0,2,1:T(4,128)S(1)}, u32[]{:S(2)}, u32[]{:S(2)}) collective-permute-start(f32[4,2,1,4096]{3,0,2,1:T(4,128)S(1)} %get-tuple-element.19), channel_id=1, source_target_pairs={{1,0},{2,1},{3,2},{4,3},{5,4},{6,5},{7,6},{9,8},{10,9},{11,10},{12... | collective-permute-start | bytes 393224 | tf_op jit(solution)/shard_map/ppermute | solution.py:18
  468.0 13.4 %collective-permute-start.15 = (f32[4,2,1,4096]{3,0,2,1:T(4,128)S(1)}, f32[4,2,1,4096]{3,0,2,1:T(4,128)S(1)}, u32[]{:S(2)}, u32[]{:S(2)}) collective-permute-start(f32[4,2,1,4096]{3,0,2,1:T(4,128)S(1)} %get-tuple-element.78), channel_id=1, source_target_pairs={{0,1},{1,2},{2,3},{3,4},{4,5},{5,6},{6,7},{8,9},{9,10},{10,11},{11... | collective-permute-start | bytes 393224 | tf_op jit(solution)/shard_map/ppermute | solution.py:17
  469.9 11.5 %collective-permute-start.14 = (f32[4,2,1,4096]{3,0,2,1:T(4,128)S(1)}, f32[4,2,1,4096]{3,0,2,1:T(4,128)S(1)}, u32[]{:S(2)}, u32[]{:S(2)}) collective-permute-start(f32[4,2,1,4096]{3,0,2,1:T(4,128)S(1)} %get-tuple-element.79), channel_id=1, source_target_pairs={{1,0},{2,1},{3,2},{4,3},{5,4},{6,5},{7,6},{9,8},{10,9},{11,10},{12... | collective-permute-start | bytes 393224 | tf_op jit(solution)/shard_map/ppermute | solution.py:18
  475.8 15.6 %collective-permute-start.47 = (f32[4,2,1,4096]{3,0,2,1:T(4,128)S(1)}, f32[4,2,1,4096]{3,0,2,1:T(4,128)S(1)}, u32[]{:S(2)}, u32[]{:S(2)}) collective-permute-start(f32[4,2,1,4096]{3,0,2,1:T(4,128)S(1)} %get-tuple-element.14), channel_id=1, source_target_pairs={{0,1},{1,2},{2,3},{3,4},{4,5},{5,6},{6,7},{8,9},{9,10},{10,11},{11... | collective-permute-start | bytes 393224 | tf_op jit(solution)/shard_map/ppermute | solution.py:17
  477.7 13.6 %collective-permute-start.46 = (f32[4,2,1,4096]{3,0,2,1:T(4,128)S(1)}, f32[4,2,1,4096]{3,0,2,1:T(4,128)S(1)}, u32[]{:S(2)}, u32[]{:S(2)}) collective-permute-start(f32[4,2,1,4096]{3,0,2,1:T(4,128)S(1)} %get-tuple-element.15), channel_id=1, source_target_pairs={{1,0},{2,1},{3,2},{4,3},{5,4},{6,5},{7,6},{9,8},{10,9},{11,10},{12... | collective-permute-start | bytes 393224 | tf_op jit(solution)/shard_map/ppermute | solution.py:18
  484.6 14.3 %collective-permute-start.17 = (f32[4,2,1,4096]{3,0,2,1:T(4,128)S(1)}, f32[4,2,1,4096]{3,0,2,1:T(4,128)S(1)}, u32[]{:S(2)}, u32[]{:S(2)}) collective-permute-start(f32[4,2,1,4096]{3,0,2,1:T(4,128)S(1)} %get-tuple-element.74), channel_id=1, source_target_pairs={{0,1},{1,2},{2,3},{3,4},{4,5},{5,6},{6,7},{8,9},{9,10},{10,11},{11... | collective-permute-start | bytes 393224 | tf_op jit(solution)/shard_map/ppermute | solution.py:17
  486.6 12.4 %collective-permute-start.16 = (f32[4,2,1,4096]{3,0,2,1:T(4,128)S(1)}, f32[4,2,1,4096]{3,0,2,1:T(4,128)S(1)}, u32[]{:S(2)}, u32[]{:S(2)}) collective-permute-start(f32[4,2,1,4096]{3,0,2,1:T(4,128)S(1)} %get-tuple-element.75), channel_id=1, source_target_pairs={{1,0},{2,1},{3,2},{4,3},{5,4},{6,5},{7,6},{9,8},{10,9},{11,10},{12... | collective-permute-start | bytes 393224 | tf_op jit(solution)/shard_map/ppermute | solution.py:18
  502.1 8.5 %collective-permute-start.19 = (f32[4,2,1,4096]{3,0,2,1:T(4,128)}, f32[4,2,1,4096]{3,0,2,1:T(4,128)S(1)}, u32[]{:S(2)}, u32[]{:S(2)}) collective-permute-start(f32[4,2,1,4096]{3,0,2,1:T(4,128)} %get-tuple-element.70), channel_id=1, source_target_pairs={{0,1},{1,2},{2,3},{3,4},{4,5},{5,6},{6,7},{8,9},{9,10},{10,11},{11... | collective-permute-start | bytes 393224 | tf_op jit(solution)/shard_map/ppermute | solution.py:17
  504.1 6.6 collective-permute-start.18
  512.9 7.2 collective-permute-start.21
  515.2 6.6 collective-permute-start.20
  523.9 10.8 %collective-permute-start.23 = (f32[4,2,1,4096]{3,0,2,1:T(4,128)S(1)}, f32[4,2,1,4096]{3,0,2,1:T(4,128)S(1)}, u32[]{:S(2)}, u32[]{:S(2)}) collective-permute-start(f32[4,2,1,4096]{3,0,2,1:T(4,128)S(1)} %get-tuple-element.62), channel_id=1, source_target_pairs={{0,1},{1,2},{2,3},{3,4},{4,5},{5,6},{6,7},{8,9},{9,10},{10,11},{11... | collective-permute-start | bytes 393224 | tf_op jit(solution)/shard_map/ppermute | solution.py:17
  527.9 6.9 collective-permute-start.22
  (6 other events, 30.3 us)
Sparse Core Ops, SparseCore 0:
  12.4 114.3 all-gather.7
  130.2 105.4 all-gather.5
  239.2 105.4 all-gather.3
  510.8 230.2 reduce-scatter.1
